TPU v7x, 32 devices: a whole 2x2x4 slice. The times are simulated.
32 devices in a mesh: dp: 8 (over z, y), mp: 4 (over x, core).
Axes of the slice: x: 2, y: 2, z: 4, core: 2. Of those that a mesh axis runs over, the one named last changes fastest.
Arguments:
- tokens: bfloat16 [8192, 768], P(('dp', 'mp')), may hold values from -6 to 6
- segment_ids: int32 [8192], P('dp'), may hold values from 0 to 10, as said below
- keep_mask: int32 [88, 2], P('dp'), may hold values 0 or 1
- first_gain: bfloat16 [768], replicated, may hold values from 0.5 to 1.5
- first_shift: bfloat16 [768], replicated, may hold values from -3 to 3
- query_weight: bfloat16 [768, 768], P(None, 'mp'), may hold values from -0.21875 to 0.21875
- query_bias: bfloat16 [768], P('mp'), may hold values from -3 to 3
- key_weight: bfloat16 [768, 768], P(None, 'mp'), may hold values from -0.21875 to 0.21875
- value_weight: bfloat16 [768, 768], P(None, 'mp'), may hold values from -0.21875 to 0.21875
- value_bias: bfloat16 [768], P('mp'), may hold values from -3 to 3
- out_weight: bfloat16 [768, 768], P('mp'), may hold values from -2.5 to 2.5
- out_bias: bfloat16 [768], replicated, may hold values from -2 to 2
- second_gain: bfloat16 [768], replicated, may hold values from 0.5 to 1.5
- second_shift: bfloat16 [768], replicated, may hold values from -3 to 3
- up_weight: bfloat16 [768, 3072], P(None, 'mp'), may hold values from -0.21875 to 0.21875
- up_bias: bfloat16 [3072], P('mp'), may hold values from -3 to 3
- down_weight: bfloat16 [3072, 768], P('mp'), may hold values from -0.109375 to 0.109375
- down_bias: bfloat16 [768], replicated, may hold values from -2 to 2
- cotangent: bfloat16 [8192, 768], P(('dp', 'mp')), may hold values from -6 to 6
Outputs:
- layer_out: bfloat16 [8192, 768], P(('dp', 'mp'))
- input_grad: float32 [8192, 768], P(('dp', 'mp'))
- first_gain_grad: float32 [768], replicated
- first_shift_grad: float32 [768], replicated
- query_weight_grad: float32 [768, 768], P(None, 'mp')
- query_bias_grad: float32 [768], P('mp')
- key_weight_grad: float32 [768, 768], P(None, 'mp')
- value_weight_grad: float32 [768, 768], P(None, 'mp')
- value_bias_grad: float32 [768], P('mp')
- out_weight_grad: float32 [768, 768], P('mp')
- out_bias_grad: float32 [768], replicated
- second_gain_grad: float32 [768], replicated
- second_shift_grad: float32 [768], replicated
- up_weight_grad: float32 [768, 3072], P(None, 'mp')
- up_bias_grad: float32 [3072], P('mp')
- down_weight_grad: float32 [3072, 768], P('mp')
- down_bias_grad: float32 [768], replicated
Inputs may be any that keep to these rules, and one draw needn't show every extreme that they name: `segment_ids`: within each aligned block of 1024 tokens the ids start at 0, never fall and rise by one from image to image; every image but the last of a block has 102, 198 or 578 tokens, the last holds the remaining tokens. In the first block every image but the last has 102 tokens. `keep_mask`: row i of a block of 11 rows belongs to the image with segment id i of the same index of dp.
All inputs are finite; a program needn't handle non-finite values.
Results may differ from a plain program's by a relative error of at most 0.02.
Values may be sent and summed in bfloat16 or wider, within the bound.
No kernel may reach another device: no remote copies, remote signals or barrier semaphores. Data moves between devices by JAX's collectives and lax.ppermute only.
A program may use at most 128 MiB of HBM per device.

v0:
```python
import math
import jax
import jax.numpy as jnp
from jax import lax
from jax.sharding import PartitionSpec as P

HD = 64
eps = 1e-06


def layer_norm(values, scaling, bias_add):
    center = values - jnp.mean(values, axis=-1, keepdims=True)
    spread = jnp.mean(center * center, axis=-1, keepdims=True)
    return center * lax.rsqrt(spread + eps) * scaling + bias_add


def gelu_exact(values):
    return jax.nn.gelu(values, approximate=False)


def per_device(
    tokens,
    segment_ids,
    keep_mask,
    first_gain,
    first_shift,
    query_weight,
    query_bias,
    key_weight,
    value_weight,
    value_bias,
    out_weight,
    out_bias,
    second_gain,
    second_shift,
    up_weight,
    up_bias,
    down_weight,
    down_bias,
    cotangent,
):
    f32 = jnp.float32
    bf16 = jnp.bfloat16
    local_rows = tokens.shape[0]
    row_count = segment_ids.shape[0]
    head_width = query_weight.shape[1]
    head_group = head_width // HD
    score_scale = 1.0 / math.sqrt(HD)
    block_rows = min(512, row_count)
    block_count = row_count // block_rows
    offset = lax.axis_index("mp") * local_rows
    local_ids = lax.dynamic_slice_in_dim(segment_ids, offset, local_rows)
    onehot = (
        local_ids[:, None] == jnp.arange(keep_mask.shape[0], dtype=jnp.int32)[None, :]
    ).astype(f32)
    keep_rows = jnp.dot(onehot, keep_mask.astype(f32), precision=lax.Precision.HIGHEST) / 0.9
    allowed = segment_ids[:, None] == segment_ids[None, :]
    gain_one = first_gain.astype(f32)
    shift_one = first_shift.astype(f32)
    gain_two = second_gain.astype(f32)
    shift_two = second_shift.astype(f32)
    inputs = tokens.astype(f32)
    normed = layer_norm(inputs, gain_one, shift_one).astype(bf16)
    normed_all = lax.all_gather(normed, "mp", axis=0, tiled=True)
    query_rows = (
        jnp.dot(normed_all, query_weight, preferred_element_type=f32) + query_bias.astype(f32)
    ).astype(bf16)
    key_rows = jnp.dot(normed_all, key_weight, preferred_element_type=f32).astype(bf16)
    value_rows = (
        jnp.dot(normed_all, value_weight, preferred_element_type=f32) + value_bias.astype(f32)
    ).astype(bf16)
    key_heads = key_rows.reshape(row_count, head_group, HD)
    value_heads = value_rows.reshape(row_count, head_group, HD)
    context_parts = []
    lse_parts = []
    for number in range(block_count):
        row_start = number * block_rows
        query_block = query_rows[row_start : row_start + block_rows].reshape(
            block_rows, head_group, HD
        )
        scores = (
            jnp.einsum("qhd,khd->hqk", query_block, key_heads, preferred_element_type=f32)
            * score_scale
        )
        scores = jnp.where(allowed[row_start : row_start + block_rows][None], scores, -1e30)
        largest = jnp.max(scores, axis=-1, keepdims=True)
        powers = jnp.exp(scores - largest)
        totals = jnp.sum(powers, axis=-1, keepdims=True)
        weights = (powers / totals).astype(bf16)
        context_block = jnp.einsum("hqk,khd->qhd", weights, value_heads, preferred_element_type=f32)
        context_parts.append(context_block.reshape(block_rows, head_width))
        lse_parts.append(largest + jnp.log(totals))
    context = jnp.concatenate(context_parts, axis=0).astype(bf16)
    attended = lax.psum_scatter(
        jnp.dot(context, out_weight, preferred_element_type=f32).astype(jnp.bfloat16),
        "mp",
        scatter_dimension=0,
        tiled=True,
    ).astype(jnp.float32) + out_bias.astype(f32)
    middle = inputs + keep_rows[:, 0:1] * attended
    normed_two = layer_norm(middle, gain_two, shift_two).astype(bf16)
    normed_two_all = lax.all_gather(normed_two, "mp", axis=0, tiled=True)
    hidden = jnp.dot(normed_two_all, up_weight, preferred_element_type=f32) + up_bias.astype(f32)
    activated = gelu_exact(hidden).astype(bf16)
    mlp_out = lax.psum_scatter(
        jnp.dot(activated, down_weight, preferred_element_type=f32).astype(jnp.bfloat16),
        "mp",
        scatter_dimension=0,
        tiled=True,
    ).astype(jnp.float32) + down_bias.astype(f32)
    layer_out = (middle + keep_rows[:, 1:2] * mlp_out).astype(bf16)
    out_grad = cotangent.astype(f32)
    mlp_grad = out_grad * keep_rows[:, 1:2]
    down_bias_grad = jnp.sum(mlp_grad, axis=0)
    mlp_grad_all = lax.all_gather(mlp_grad.astype(bf16), "mp", axis=0, tiled=True)
    down_weight_grad = jnp.einsum("rf,rd->fd", activated, mlp_grad_all, preferred_element_type=f32)
    act_grad = jnp.einsum("rd,fd->rf", mlp_grad_all, down_weight, preferred_element_type=f32)
    unused_value, gelu_pull = jax.vjp(gelu_exact, hidden)
    hidden_grad = gelu_pull(act_grad)[0].astype(bf16)
    up_bias_grad = jnp.sum(hidden_grad.astype(f32), axis=0)
    up_weight_grad = jnp.einsum(
        "rd,rf->df", normed_two_all, hidden_grad, preferred_element_type=f32
    )
    second_grad = lax.psum_scatter(
        jnp.einsum("rf,df->rd", hidden_grad, up_weight, preferred_element_type=f32).astype(
            jnp.bfloat16
        ),
        "mp",
        scatter_dimension=0,
        tiled=True,
    ).astype(jnp.float32)
    unused_value, norm_pull_two = jax.vjp(layer_norm, middle, gain_two, shift_two)
    middle_part, gain_two_grad, shift_two_grad = norm_pull_two(second_grad)
    middle_grad = out_grad + middle_part
    attn_grad = middle_grad * keep_rows[:, 0:1]
    out_bias_grad = jnp.sum(attn_grad, axis=0)
    attn_grad_all = lax.all_gather(attn_grad.astype(bf16), "mp", axis=0, tiled=True)
    out_weight_grad = jnp.einsum("rc,rd->cd", context, attn_grad_all, preferred_element_type=f32)
    context_grad = jnp.einsum(
        "rd,cd->rc", attn_grad_all, out_weight, preferred_element_type=f32
    ).astype(bf16)
    context_grad_heads = context_grad.reshape(row_count, head_group, HD)
    query_grads = []
    key_grad = jnp.zeros((row_count, head_group, HD), f32)
    value_grad = jnp.zeros((row_count, head_group, HD), f32)
    for number in range(block_count):
        row_start = number * block_rows
        query_block = query_rows[row_start : row_start + block_rows].reshape(
            block_rows, head_group, HD
        )
        scores = (
            jnp.einsum("qhd,khd->hqk", query_block, key_heads, preferred_element_type=f32)
            * score_scale
        )
        scores = jnp.where(allowed[row_start : row_start + block_rows][None], scores, -1e30)
        probs = jnp.exp(scores - lse_parts[number])
        grad_block = context_grad_heads[row_start : row_start + block_rows]
        prob_grad = jnp.einsum("qhd,khd->hqk", grad_block, value_heads, preferred_element_type=f32)
        center = jnp.sum(probs * prob_grad, axis=-1, keepdims=True)
        score_grad = (probs * (prob_grad - center)).astype(bf16)
        query_grads.append(
            jnp.einsum("hqk,khd->qhd", score_grad, key_heads, preferred_element_type=f32)
            * score_scale
        )
        key_grad = (
            key_grad
            + jnp.einsum("hqk,qhd->khd", score_grad, query_block, preferred_element_type=f32)
            * score_scale
        )
        value_grad = value_grad + jnp.einsum(
            "hqk,qhd->khd", probs.astype(bf16), grad_block, preferred_element_type=f32
        )
    query_grad_rows = (
        jnp.concatenate(query_grads, axis=0).reshape(row_count, head_width).astype(bf16)
    )
    key_grad_rows = key_grad.reshape(row_count, head_width).astype(bf16)
    value_grad_rows = value_grad.reshape(row_count, head_width).astype(bf16)
    query_bias_grad = jnp.sum(query_grad_rows.astype(f32), axis=0)
    value_bias_grad = jnp.sum(value_grad_rows.astype(f32), axis=0)
    query_weight_grad = jnp.einsum(
        "rd,rc->dc", normed_all, query_grad_rows, preferred_element_type=f32
    )
    key_weight_grad = jnp.einsum("rd,rc->dc", normed_all, key_grad_rows, preferred_element_type=f32)
    value_weight_grad = jnp.einsum(
        "rd,rc->dc", normed_all, value_grad_rows, preferred_element_type=f32
    )
    total = jnp.einsum("rc,dc->rd", query_grad_rows, query_weight, preferred_element_type=f32)
    total = total + jnp.einsum("rc,dc->rd", key_grad_rows, key_weight, preferred_element_type=f32)
    first_grad = lax.psum_scatter(
        (
            total
            + jnp.einsum("rc,dc->rd", value_grad_rows, value_weight, preferred_element_type=f32)
        ).astype(jnp.bfloat16),
        "mp",
        scatter_dimension=0,
        tiled=True,
    ).astype(jnp.float32)
    unused_value, norm_pull_one = jax.vjp(layer_norm, inputs, gain_one, shift_one)
    input_part, gain_one_grad, shift_one_grad = norm_pull_one(first_grad)
    input_grad = middle_grad + input_part
    (
        query_weight_grad,
        query_bias_grad,
        key_weight_grad,
        value_weight_grad,
        value_bias_grad,
        out_weight_grad,
        up_weight_grad,
        up_bias_grad,
        down_weight_grad,
    ) = lax.psum(
        (
            query_weight_grad,
            query_bias_grad,
            key_weight_grad,
            value_weight_grad,
            value_bias_grad,
            out_weight_grad,
            up_weight_grad,
            up_bias_grad,
            down_weight_grad,
        ),
        "dp",
    )
    gain_one_grad, shift_one_grad, out_bias_grad, gain_two_grad, shift_two_grad, down_bias_grad = (
        lax.psum(
            (
                gain_one_grad,
                shift_one_grad,
                out_bias_grad,
                gain_two_grad,
                shift_two_grad,
                down_bias_grad,
            ),
            ("dp", "mp"),
        )
    )
    return (
        layer_out,
        input_grad,
        gain_one_grad,
        shift_one_grad,
        query_weight_grad,
        query_bias_grad,
        key_weight_grad,
        value_weight_grad,
        value_bias_grad,
        out_weight_grad,
        out_bias_grad,
        gain_two_grad,
        shift_two_grad,
        up_weight_grad,
        up_bias_grad,
        down_weight_grad,
        down_bias_grad,
    )


def solution(mesh):
    in_specs = (
        P(("dp", "mp"), None),
        P("dp"),
        P("dp", None),
        P(),
        P(),
        P(None, "mp"),
        P("mp"),
        P(None, "mp"),
        P(None, "mp"),
        P("mp"),
        P("mp", None),
        P(),
        P(),
        P(),
        P(None, "mp"),
        P("mp"),
        P("mp", None),
        P(),
        P(("dp", "mp"), None),
    )
    out_specs = (
        P(("dp", "mp"), None),
        P(("dp", "mp"), None),
        P(),
        P(),
        P(None, "mp"),
        P("mp"),
        P(None, "mp"),
        P(None, "mp"),
        P("mp"),
        P("mp", None),
        P(),
        P(),
        P(),
        P(None, "mp"),
        P("mp"),
        P("mp", None),
        P(),
    )
    return jax.shard_map(
        per_device, mesh=mesh, in_specs=in_specs, out_specs=out_specs, check_vma=False
    )
```

profile of v0, /device:TPU:0, one launch (start us, length us, event | category | flops | bytes accessed | tf_op | source)
XLA Modules:
  0.0 535.1 jit_solution(10001136210454369403)
XLA Ops:
  11.7 2.0 fusion.43
  15.1 1.4 broadcast_compare_fusion
  17.6 18.7 %all-gather.5.cloned.1.call-done = bf16[1024,768]{1,0:T(8,128)(2,1)} async-done(((bf16[256,768]{1,0:T(8,128)(2,1)}), bf16[1024,768]{1,0:T(8,128)(2,1)}) %all-gather.5.cloned.1.call-update) | async-done | bytes 1572880 | tf_op jit(solution)/shard_map/all_gather | solution.py:64
  36.2 2.3 fusion.27
  39.3 1.4 fusion.65
  40.7 1.5 fusion
  43.3 1.6 fusion.35
  45.0 1.4 fusion.64
  46.5 1.5 fusion.1
  49.7 1.7 fusion.34
  52.0 1.8 convolution_convert_fusion.2
  58.1 23.9 %reduce-scatter.5.cloned.1.call-done = bf16[256,768]{1,0:T(8,128)(2,1)} async-done(((bf16[1024,768]{1,0:T(8,128)(2,1)}), bf16[256,768]{1,0:T(8,128)(2,1)}) %reduce-scatter.5.cloned.1.call-update) | async-done | bytes 393232 | tf_op jit(solution)/shard_map/reduce_scatter | solution.py:94
  83.3 1.3 multiply_reduce_fusion.2
  85.9 2.0 add_convert_fusion.3
  88.0 1.6 fusion.37
  90.8 16.9 %all-gather.7.cloned.1.call-done = bf16[1024,768]{1,0:T(8,128)(2,1)} async-done(((bf16[256,768]{1,0:T(8,128)(2,1)}), bf16[1024,768]{1,0:T(8,128)(2,1)}) %all-gather.7.cloned.1.call-update) | async-done | bytes 1572880 | tf_op jit(solution)/shard_map/all_gather | solution.py:102
  107.7 4.8 fusion.66
  112.5 16.9 %all-gather.9.cloned.1.call-done = bf16[1024,768]{1,0:T(8,128)(2,1)} async-done(((bf16[256,768]{1,0:T(8,128)(2,1)}), bf16[1024,768]{1,0:T(8,128)(2,1)}) %all-gather.9.cloned.1.call-update) | async-done | bytes 1572880 | tf_op jit(solution)/shard_map/all_gather | solution.py:115
  129.4 11.8 %convert_reduce_fusion = (f32[768]{0:T(1024)}, bf16[1024,768]{1,0:T(8,128)(2,1)S(1)}, f32[1024,768]{1,0:T(8,128)}) fusion(f32[1024,768]{1,0:T(8,128)} %fusion.66, f32[768]{0:T(1024)S(1)} %convert_element_type.170, bf16[1024,768]{1,0:T(8,128)(2,1)} %all-gather.9.cloned.1.call-done, bf16[768,768]{1,0:T(8,128)(2,1)S(1)} %copy-done), kind=kOutput, calls=%fused_computation.20 | convolution fusion | flops 1266941184 | bytes 10622976 | tf_op jit(solution)/shard_map/rd,fd->rf/dot_general | solution.py:117
  142.4 2.6 convolution_convert_fusion
  145.0 3.3 multiply_convert_fusion.2
  149.5 2.5 convolution_convert_fusion.1
  152.1 1.4 convert_element_type.174
  153.5 19.7 %reduce-scatter.9.cloned.1.call-done = bf16[256,768]{1,0:T(8,128)(2,1)} async-done(((bf16[1024,768]{1,0:T(8,128)(2,1)}), bf16[256,768]{1,0:T(8,128)(2,1)}) %reduce-scatter.9.cloned.1.call-update) | async-done | bytes 393232 | tf_op jit(solution)/shard_map/reduce_scatter | solution.py:124
  173.1 2.1 fusion.47
  176.5 27.7 %reduce-scatter.7.cloned.1.call-done = bf16[256,768]{1,0:T(8,128)(2,1)} async-done(((bf16[1024,768]{1,0:T(8,128)(2,1)}), bf16[256,768]{1,0:T(8,128)(2,1)}) %reduce-scatter.7.cloned.1.call-update) | async-done | bytes 393232 | tf_op jit(solution)/shard_map/reduce_scatter | solution.py:105
  204.2 2.6 fusion.59
  206.8 2.4 fusion.36
  210.8 18.1 %all-gather.11.cloned.1.call-done = bf16[1024,768]{1,0:T(8,128)(2,1)} async-done(((bf16[256,768]{1,0:T(8,128)(2,1)}), bf16[1024,768]{1,0:T(8,128)(2,1)}) %all-gather.11.cloned.1.call-update) | async-done | bytes 1572880 | tf_op jit(solution)/shard_map/all_gather | solution.py:137
  229.0 2.1 convolution_convert_fusion.3
  231.1 3.9 multiply_reduce_fusion.1
  235.8 1.4 multiply_convert_fusion.1
  240.2 1.9 multiply_reduce_fusion
  242.1 1.8 convert_reduce_fusion.4
  244.0 1.4 multiply_convert_fusion
  249.6 1.8 add_convert_fusion
  251.7 4.9 fusion.71
  256.6 2.8 fusion.70
  265.5 22.2 %all-reduce.1 = (f32[192]{0:T(256)}, f32[192]{0:T(256)}, f32[768]{0:T(1024)}) all-reduce(f32[192]{0:T(256)S(1)} %reduce_sum.217, f32[192]{0:T(256)S(1)} %reduce_sum.219, f32[768]{0:T(1024)S(1)} %copy-done.58), channel_id=1, replica_groups=mesh['dp'=8,'mp'=4] {'dp'}, use_global_device_ids=true, to_apply=%region_24.25 | all-reduce | flops 1152 | bytes 9216 | tf_op jit(solution)/shard_map/psum | solution.py:211
  289.0 1.5 fusion.48
  290.6 41.8 %all-reduce = (f32[768]{0:T(1024)}, f32[768]{0:T(1024)}, f32[768]{0:T(1024)}, f32[768]{0:T(1024)}, f32[768]{0:T(1024)}, /*index=5*/f32[768]{0:T(1024)}) all-reduce(f32[768]{0:T(1024)S(1)} %get-tuple-element.19, f32[768]{0:T(1024)S(1)} %get-tuple-element.24, f32[768]{0:T(1024)S(1)} %copy-done.50, ...), channel_id=1, replica_groups=mesh['dp'=8,'mp'=4] {'dp','mp'}, use_global_device_ids=true, to_apply=%region_19.20 | all-reduce | flops 4608 | bytes 36864 | tf_op jit(solution)/shard_map/psum | solution.py:226
  332.3 2.3 add_add_fusion.2
  334.6 184.2 %all-reduce.5.cloned.1.call-done = (f32[768,192]{0,1:T(8,128)}, f32[768,192]{0,1:T(8,128)}, f32[768,192]{0,1:T(8,128)}, f32[192,768]{1,0:T(8,128)}, f32[768,768]{1,0:T(8,128)}, /*index=5*/f32[768,768]{1,0:T(8,128)}) async-done(((f32[768,192]{0,1:T(8,128)}, f32[768,192]{0,1:T(8,128)}, f32[768,192]{0,1:T(8,128)}, f32[192,768]{1,0:T(8,128)}, f32[768,768]{1,0:T(8,128)}, /*index=5*/f32[768,768]{1,0:T(8,128)}), ...) | async-done | bytes 7077904 | tf_op jit(solution)/shard_map/psum | solution.py:211
  518.8 2.1 copy.42
  520.9 1.9 copy.43
  522.8 1.9 copy.44
  525.6 1.4 copy.46
  527.0 1.4 copy.47
  (202 shorter events, 40.8 us)
Async XLA Ops:
  7.2 122.2 %copy-start = (bf16[768,768]{1,0:T(8,128)(2,1)S(1)}, bf16[768,768]{1,0:T(8,128)(2,1)}, u32[]{:S(2)}) copy-start(bf16[768,768]{1,0:T(8,128)(2,1)} %param.35) | copy-start | bytes 3538948
  7.2 29.0 %all-gather.5.cloned.1.call-start = ((), (), s32[]{:S(2)}) async-start(), calls=%async_computation.4 | async-start | bytes 1966080 | tf_op jit(solution)/shard_map/all_gather | solution.py:64
  8.5 6.0 %copy-start.40 = (f32[256]{0:T(256)}, f32[256]{0:T(256)S(1)}, u32[]{:S(2)}) copy-start(f32[256]{0:T(256)S(1)} %broadcast_multiply_fusion.1) | copy-start | bytes 3076
  10.3 4.1 copy-start.45
  11.0 3.4 copy-start.37
  13.7 68.3 %reduce-scatter.5.cloned.1.call-start = ((), (), s32[]{:S(2)}) async-start(), calls=%async_computation.5 | async-start | bytes 1966080 | tf_op jit(solution)/shard_map/reduce_scatter | solution.py:94
  15.1 23.4 %copy-start.34 = (bf16[768,192]{0,1:T(8,128)(2,1)S(1)}, bf16[768,192]{0,1:T(8,128)(2,1)}, u32[]{:S(2)}) copy-start(bf16[768,192]{0,1:T(8,128)(2,1)} %param.26) | copy-start | bytes 884740
  36.2 3.0 copy-start.19
  38.6 6.5 %copy-start.16 = (bf16[512,192]{0,1:T(8,128)(2,1)}, bf16[512,192]{0,1:T(8,128)(2,1)S(1)}, u32[]{:S(2)}) copy-start(bf16[512,192]{0,1:T(8,128)(2,1)S(1)} %get-tuple-element.55) | copy-start | bytes 589828
  39.2 5.8 %copy-start.7 = (bf16[1024,192]{0,1:T(8,128)(2,1)}, bf16[1024,192]{0,1:T(8,128)(2,1)S(1)}, u32[]{:S(2)}) copy-start(bf16[1024,192]{0,1:T(8,128)(2,1)S(1)} %convolution_convert_fusion.4) | copy-start | bytes 1179652
  42.9 5.1 copy-start.22
  45.0 6.4 %copy-start.26 = (bf16[3,64,512]{2,1,0:T(8,128)(2,1)}, bf16[3,64,512]{2,1,0:T(8,128)(2,1)S(1)}, u32[]{:S(2)}) copy-start(bf16[3,64,512]{2,1,0:T(8,128)(2,1)S(1)} %fusion.35) | copy-start | bytes 589828
  51.4 3.3 copy-start.59
  51.4 30.7 %copy-start.4 = (bf16[256,768]{1,0:T(8,128)(2,1)S(1)}, bf16[256,768]{1,0:T(8,128)(2,1)}, u32[]{:S(2)}) copy-start(bf16[256,768]{1,0:T(8,128)(2,1)} %param.19) | copy-start | bytes 1179652
  52.0 35.9 %copy-start.11 = (bf16[256,768]{1,0:T(8,128)(2,1)S(1)}, bf16[256,768]{1,0:T(8,128)(2,1)}, u32[]{:S(2)}) copy-start(bf16[256,768]{1,0:T(8,128)(2,1)} %param.37) | copy-start | bytes 1179652
  53.8 53.9 %all-gather.7.cloned.1.call-start = ((), (), s32[]{:S(2)}) async-start(), calls=%async_computation.6 | async-start | bytes 1966080 | tf_op jit(solution)/shard_map/all_gather | solution.py:102
  87.9 41.4 %all-gather.9.cloned.1.call-start = ((), (), s32[]{:S(2)}) async-start(), calls=%async_computation.8 | async-start | bytes 1966080 | tf_op jit(solution)/shard_map/all_gather | solution.py:115
  89.6 83.6 %reduce-scatter.9.cloned.1.call-start = ((), (), s32[]{:S(2)}) async-start(), calls=%async_computation.9 | async-start | bytes 1966080 | tf_op jit(solution)/shard_map/reduce_scatter | solution.py:124
  129.4 13.0 %copy-start.61 = (bf16[768,768]{1,0:T(8,128)(2,1)S(1)}, bf16[768,768]{1,0:T(8,128)(2,1)}, u32[]{:S(2)}) copy-start(bf16[768,768]{1,0:T(8,128)(2,1)} %param.33) | copy-start | bytes 3538948
  145.0 59.2 %reduce-scatter.7.cloned.1.call-start = ((), (), s32[]{:S(2)}) async-start(), calls=%async_computation.7 | async-start | bytes 1966080 | tf_op jit(solution)/shard_map/reduce_scatter | solution.py:105
  149.5 23.7 %copy-start.6 = (bf16[256,768]{1,0:T(8,128)(2,1)S(1)}, bf16[256,768]{1,0:T(8,128)(2,1)}, u32[]{:S(2)}) copy-start(bf16[256,768]{1,0:T(8,128)(2,1)} %reduce-scatter.5.cloned.1.call-done) | copy-start | bytes 1179652
  152.0 54.8 %copy-start.12 = (bf16[256,768]{1,0:T(8,128)(2,1)S(1)}, bf16[256,768]{1,0:T(8,128)(2,1)}, u32[]{:S(2)}) copy-start(bf16[256,768]{1,0:T(8,128)(2,1)} %param.37) | copy-start | bytes 1179652
  152.0 76.9 %all-gather.11.cloned.1.call-start = ((), (), s32[]{:S(2)}) async-start(), calls=%async_computation.10 | async-start | bytes 1966080 | tf_op jit(solution)/shard_map/all_gather | solution.py:137
  206.8 24.3 %copy-start.23 = (bf16[1024,192]{0,1:T(8,128)(2,1)S(1)}, bf16[1024,192]{0,1:T(8,128)(2,1)}, u32[]{:S(2)}) copy-start(bf16[1024,192]{0,1:T(8,128)(2,1)} %copy-done.22) | copy-start | bytes 1179652
  209.2 78.5 %reduce-scatter.11.cloned.1.call-start = ((), (), s32[]{:S(2)}) async-start(), calls=%async_computation.11 | async-start | bytes 1966080 | tf_op jit(solution)/shard_map/reduce_scatter | solution.py:189
  231.1 4.0 slice-start
  231.1 4.7 slice-start.1
  235.1 3.9 slice-start.2
  235.8 3.2 slice-start.3
  251.4 267.4 %all-reduce.5.cloned.1.call-start = ((), (), s32[]{:S(2)}) async-start(), calls=%async_computation.12 | async-start | bytes 14155776 | tf_op jit(solution)/shard_map/psum | solution.py:211
  251.7 4.9 copy-start.60
  251.7 4.9 copy-start.63
  256.6 2.9 copy-start.25
  256.6 2.9 copy-start.27
  256.6 2.9 copy-start.29
  264.7 23.0 %copy-start.38 = (f32[768]{0:T(1024)S(1)}, f32[768]{0:T(1024)}, u32[]{:S(2)}) copy-start(f32[768]{0:T(1024)} %copy-done.37) | copy-start | bytes 9220
  264.7 23.0 %copy-start.41 = (f32[256]{0:T(256)S(1)}, f32[256]{0:T(256)}, u32[]{:S(2)}) copy-start(f32[256]{0:T(256)} %copy-done.40) | copy-start | bytes 3076
  264.7 24.3 %copy-start.55 = (f32[256]{0:T(256)S(1)}, f32[256]{0:T(256)}, u32[]{:S(2)}) copy-start(f32[256]{0:T(256)} %copy-done.54) | copy-start | bytes 3076
  264.7 24.3 %copy-start.46 = (f32[256]{0:T(256)S(1)}, f32[256]{0:T(256)}, u32[]{:S(2)}) copy-start(f32[256]{0:T(256)} %copy-done.45) | copy-start | bytes 3076
  264.7 25.8 %copy-start.47 = (f32[768]{0:T(1024)S(1)}, f32[768]{0:T(1024)}, u32[]{:S(2)}) copy-start(f32[768]{0:T(1024)} %get-tuple-element.17) | copy-start | bytes 9220
  264.7 25.8 %copy-start.48 = (f32[768]{0:T(1024)S(1)}, f32[768]{0:T(1024)}, u32[]{:S(2)}) copy-start(f32[768]{0:T(1024)} %get-tuple-element.23) | copy-start | bytes 9220
  264.7 25.8 %copy-start.49 = (f32[768]{0:T(1024)S(1)}, f32[768]{0:T(1024)}, u32[]{:S(2)}) copy-start(f32[768]{0:T(1024)} %get-tuple-element.21) | copy-start | bytes 9220
  264.7 25.8 %copy-start.50 = (f32[768]{0:T(1024)S(1)}, f32[768]{0:T(1024)}, u32[]{:S(2)}) copy-start(f32[768]{0:T(1024)} %get-tuple-element.22) | copy-start | bytes 9220
  264.7 67.6 %copy-start.13 = (bf16[256,768]{1,0:T(8,128)(2,1)S(1)}, bf16[256,768]{1,0:T(8,128)(2,1)}, u32[]{:S(2)}) copy-start(bf16[256,768]{1,0:T(8,128)(2,1)} %param.37) | copy-start | bytes 1179652
  264.8 67.6 %copy-start.53 = (f32[256]{0:T(256)S(1)}, f32[256]{0:T(256)}, u32[]{:S(2)}) copy-start(f32[256]{0:T(256)} %copy-done.52) | copy-start | bytes 3076
  518.8 5.9 %copy-start.30 = (f32[192,768]{1,0:T(8,128)S(1)}, f32[192,768]{1,0:T(8,128)}, u32[]{:S(2)}) copy-start(f32[192,768]{1,0:T(8,128)} %get-tuple-element.77) | copy-start | bytes 1769476
  518.8 6.7 %copy-start.15 = (f32[768,768]{1,0:T(8,128)S(1)}, f32[768,768]{1,0:T(8,128)}, u32[]{:S(2)}) copy-start(f32[768,768]{1,0:T(8,128)} %get-tuple-element.81) | copy-start | bytes 7077892
  525.6 2.8 copy-start.1
  (29 other events, 45.4 us)
Sparse Core Ops, SparseCore 0:
  13.8 22.3 all-gather.4
  54.0 28.0 reduce-scatter.4
  88.0 19.6 all-gather.6
  109.7 19.6 all-gather.8
  145.1 27.9 reduce-scatter.8
  176.1 28.0 reduce-scatter.6
  209.3 19.6 all-gather.10
  251.6 27.9 reduce-scatter.10
  285.8 232.9 all-reduce.4
where the time goes:
time: 544 us; the launch traced here: 535 us
  waiting for transfers between devices  326 us (60%)
  matrix products  64.6 us (12%)
  blocking collectives  63.9 us (12%)
  other arithmetic  42.8 us (8%)
  local copies, waits for them, and re-layouts  21.6 us (4%)
  between operations  14.8 us (3%)
    psum x1, waiting for transfers between devices, per_device(): lax.psum((query_weight_grad, query_bias_grad, key_weight_grad, value_weig...  184 us
    psum x1, blocking collectives, per_device(): lax.psum((gain_one_grad, shift_one_grad, out_bias_grad, gain_two_grad, sh...  41.8 us
    reduce_scatter x1, waiting for transfers between devices, per_device(): lax.psum_scatter(jnp.dot(activated, down_weight, preferred_element_type=f...  27.7 us
    reduce_scatter x1, waiting for transfers between devices, per_device(): lax.psum_scatter(jnp.dot(context, out_weight, preferred_element_type=f32)...  23.9 us
    psum x1, blocking collectives, per_device(): lax.psum((query_weight_grad, query_bias_grad, key_weight_grad, value_weig...  22.2 us
    reduce_scatter x1, waiting for transfers between devices, per_device(): lax.psum_scatter(jnp.einsum('rf,df->rd', hidden_grad, up_weight, preferre...  19.7 us
    unnamed x142, local copies, waits for them, and re-layouts  18.9 us
    all_gather x1, waiting for transfers between devices, per_device(): normed_all = lax.all_gather(normed, 'mp', axis=0, tiled=True)  18.7 us
  transfers between devices with their start and end apart: 9, of which 8 were waited for; matrix products, arithmetic and copies ran while one was open for 8% of the time, Pallas kernels for 0%

commit v1 on v0

--- a/solution.py
+++ b/solution.py
@@ -6,6 +6,12 @@
 
 HD = 64
 eps = 1e-06
+
+
+def joined_along(blocks, dim):
+    blocks = jnp.moveaxis(blocks, 0, dim)
+    shape = blocks.shape
+    return blocks.reshape(*shape[:dim], shape[dim] * shape[dim + 1], *shape[dim + 2 :])
 
 
 def layer_norm(values, scaling, bias_add):
@@ -99,7 +105,14 @@
     ).astype(jnp.float32) + out_bias.astype(f32)
     middle = inputs + keep_rows[:, 0:1] * attended
     normed_two = layer_norm(middle, gain_two, shift_two).astype(bf16)
-    normed_two_all = lax.all_gather(normed_two, "mp", axis=0, tiled=True)
+    size = lax.axis_size("mp")
+    forward = [(i, (i + 1) % size) for i in range(size)]
+    blocks = [normed_two]
+    while len(blocks) < size:
+        blocks.append(lax.ppermute(blocks[-1], "mp", forward))
+    index = lax.axis_index("mp")
+    blocks = jnp.stack(blocks)[(index - jnp.arange(size)) % size]
+    normed_two_all = joined_along(blocks, 0)
     hidden = jnp.dot(normed_two_all, up_weight, preferred_element_type=f32) + up_bias.astype(f32)
     activated = gelu_exact(hidden).astype(bf16)
     mlp_out = lax.psum_scatter(

time: 544 us -> 538 us (0.989)
  waiting for transfers between devices: 326 us -> 318 us
    ppermute x0 -> x3, waiting for transfers between devices: none -> 26.9 us  [per_device(): blocks.append(lax.ppermute(blocks[-1], 'mp', forward))]
    all_gather x1 -> x0, waiting for transfers between devices: 16.9 us -> none  [per_device(): normed_two_all = lax.all_gather(normed_two, 'mp', axis=0, tiled=True)]
    all_gather x1, waiting for transfers between devices: 16.9 us -> 0.01 us  [per_device(): lax.all_gather(mlp_grad.astype(bf16), 'mp', axis=0, tiled=True)]
    unnamed x142 -> x144, local copies, waits for them, and re-layouts: 18.9 us -> 17.7 us
  transfers between devices with their start and end apart: 9 -> 11, of which waited for: 8 -> 9; matrix products, arithmetic and copies ran while one was open for 8% -> 10% of each run, Pallas kernels for 0% -> 0%
where the time goes in v1:
time: 538 us; the launch traced here: 529 us
  waiting for transfers between devices  318 us (59%)
  matrix products  64.6 us (12%)
  blocking collectives  64 us (12%)
  other arithmetic  42.1 us (8%)
  local copies, waits for them, and re-layouts  23.5 us (4%)
  between operations  15.2 us (3%)
    psum x1, waiting for transfers between devices, per_device(): lax.psum((query_weight_grad, query_bias_grad, key_weight_grad, value_weig...  184 us
    psum x1, blocking collectives, per_device(): lax.psum((gain_one_grad, shift_one_grad, out_bias_grad, gain_two_grad, sh...  41.8 us
    reduce_scatter x1, waiting for transfers between devices, per_device(): lax.psum_scatter(jnp.dot(activated, down_weight, preferred_element_type=f...  27.1 us
    ppermute x3, waiting for transfers between devices, per_device(): blocks.append(lax.ppermute(blocks[-1], 'mp', forward))  26.9 us
    reduce_scatter x1, waiting for transfers between devices, per_device(): lax.psum_scatter(jnp.dot(context, out_weight, preferred_element_type=f32)...  23.5 us
    psum x1, blocking collectives, per_device(): lax.psum((query_weight_grad, query_bias_grad, key_weight_grad, value_weig...  22.2 us
    reduce_scatter x1, waiting for transfers between devices, per_device(): lax.psum_scatter(jnp.einsum('rf,df->rd', hidden_grad, up_weight, preferre...  19.6 us
    all_gather x1, waiting for transfers between devices, per_device(): normed_all = lax.all_gather(normed, 'mp', axis=0, tiled=True)  18.7 us
  transfers between devices with their start and end apart: 11, of which 9 were waited for; matrix products, arithmetic and copies ran while one was open for 10% of the time, Pallas kernels for 0%

profile of v1, /device:TPU:0, one launch (start us, length us, event | category | flops | bytes accessed | tf_op | source)
XLA Modules:
  0.0 528.9 jit_solution(7641542765944824402)
XLA Ops:
  11.6 2.0 fusion.43
  15.0 1.4 broadcast_compare_fusion
  17.5 18.7 %all-gather.4.cloned.1.call-done = bf16[1024,768]{1,0:T(8,128)(2,1)} async-done(((bf16[256,768]{1,0:T(8,128)(2,1)}), bf16[1024,768]{1,0:T(8,128)(2,1)}) %all-gather.4.cloned.1.call-update) | async-done | bytes 1572880 | tf_op jit(solution)/shard_map/all_gather | solution.py:70
  36.2 2.3 fusion.27
  39.2 1.4 fusion.67
  40.7 1.5 fusion
  43.3 1.6 fusion.35
  45.0 1.4 fusion.66
  46.4 1.5 fusion.1
  49.6 1.6 fusion.34
  52.0 1.8 convolution_convert_fusion.2
  58.5 23.5 %reduce-scatter.5.cloned.1.call-done = bf16[256,768]{1,0:T(8,128)(2,1)} async-done(((bf16[1024,768]{1,0:T(8,128)(2,1)}), bf16[256,768]{1,0:T(8,128)(2,1)}) %reduce-scatter.5.cloned.1.call-update) | async-done | bytes 393232 | tf_op jit(solution)/shard_map/reduce_scatter | solution.py:100
  83.2 1.3 multiply_reduce_fusion.2
  86.0 7.2 %collective-permute-done = bf16[256,768]{1,0:T(8,128)(2,1)S(1)} collective-permute-done((bf16[256,768]{1,0:T(8,128)(2,1)S(1)}, bf16[256,768]{1,0:T(8,128)(2,1)S(1)}, u32[]{:S(2)}, u32[]{:S(2)}) %collective-permute-start) | collective-permute-done | bytes 393248 | tf_op jit(solution)/shard_map/ppermute | solution.py:112
  93.2 13.3 %collective-permute-done.1 = bf16[256,768]{1,0:T(8,128)(2,1)S(1)} collective-permute-done((bf16[256,768]{1,0:T(8,128)(2,1)S(1)}, bf16[256,768]{1,0:T(8,128)(2,1)S(1)}, u32[]{:S(2)}, u32[]{:S(2)}) %collective-permute-start.1) | collective-permute-done | bytes 393248 | tf_op jit(solution)/shard_map/ppermute | solution.py:112
  107.6 6.5 %collective-permute-done.2 = bf16[256,768]{1,0:T(8,128)(2,1)S(1)} collective-permute-done((bf16[256,768]{1,0:T(8,128)(2,1)S(1)}, bf16[256,768]{1,0:T(8,128)(2,1)S(1)}, u32[]{:S(2)}, u32[]{:S(2)}) %collective-permute-start.2) | collective-permute-done | bytes 393248 | tf_op jit(solution)/shard_map/ppermute | solution.py:112
  115.4 3.2 gather_fusion
  118.6 4.8 fusion.68
  123.4 11.9 %convert_reduce_fusion = (f32[768]{0:T(1024)}, bf16[1024,768]{1,0:T(8,128)(2,1)S(1)}, f32[1024,768]{1,0:T(8,128)}) fusion(f32[1024,768]{1,0:T(8,128)} %fusion.68, f32[768]{0:T(1024)S(1)} %convert_element_type.170, bf16[1024,768]{1,0:T(8,128)(2,1)} %all-gather.6.cloned.1.call-done, bf16[768,768]{1,0:T(8,128)(2,1)S(1)} %copy-done), kind=kOutput, calls=%fused_computation.21 | convolution fusion | flops 1266941184 | bytes 10622976 | tf_op jit(solution)/shard_map/rd,fd->rf/dot_general | solution.py:130
  136.4 2.6 convolution_convert_fusion
  139.1 3.3 multiply_convert_fusion.2
  143.5 2.6 convolution_convert_fusion.1
  146.2 1.4 convert_element_type.174
  147.6 19.6 %reduce-scatter.9.cloned.1.call-done = bf16[256,768]{1,0:T(8,128)(2,1)} async-done(((bf16[1024,768]{1,0:T(8,128)(2,1)}), bf16[256,768]{1,0:T(8,128)(2,1)}) %reduce-scatter.9.cloned.1.call-update) | async-done | bytes 393232 | tf_op jit(solution)/shard_map/reduce_scatter | solution.py:137
  167.2 2.1 fusion.47
  170.5 27.1 %reduce-scatter.7.cloned.1.call-done = bf16[256,768]{1,0:T(8,128)(2,1)} async-done(((bf16[1024,768]{1,0:T(8,128)(2,1)}), bf16[256,768]{1,0:T(8,128)(2,1)}) %reduce-scatter.7.cloned.1.call-update) | async-done | bytes 393232 | tf_op jit(solution)/shard_map/reduce_scatter | solution.py:118
  197.6 2.6 fusion.61
  200.2 2.3 fusion.36
  204.2 18.1 %all-gather.8.cloned.1.call-done = bf16[1024,768]{1,0:T(8,128)(2,1)} async-done(((bf16[256,768]{1,0:T(8,128)(2,1)}), bf16[1024,768]{1,0:T(8,128)(2,1)}) %all-gather.8.cloned.1.call-update) | async-done | bytes 1572880 | tf_op jit(solution)/shard_map/all_gather | solution.py:150
  222.4 2.1 convolution_convert_fusion.3
  224.5 3.9 multiply_reduce_fusion.1
  229.2 1.4 multiply_convert_fusion.1
  233.6 1.9 multiply_reduce_fusion
  235.6 1.8 convert_reduce_fusion.4
  237.4 1.4 multiply_convert_fusion
  243.0 1.8 add_convert_fusion
  245.1 4.9 fusion.72
  250.0 2.8 fusion.73
  258.9 22.2 %all-reduce.1 = (f32[192]{0:T(256)}, f32[192]{0:T(256)}, f32[768]{0:T(1024)}) all-reduce(f32[192]{0:T(256)S(1)} %reduce_sum.217, f32[192]{0:T(256)S(1)} %reduce_sum.219, f32[768]{0:T(1024)S(1)} %copy-done.60), channel_id=1, replica_groups=mesh['dp'=8,'mp'=4] {'dp'}, use_global_device_ids=true, to_apply=%region_24.25 | all-reduce | flops 1152 | bytes 9216 | tf_op jit(solution)/shard_map/psum | solution.py:224
  282.5 1.5 fusion.48
  284.0 41.8 %all-reduce = (f32[768]{0:T(1024)}, f32[768]{0:T(1024)}, f32[768]{0:T(1024)}, f32[768]{0:T(1024)}, f32[768]{0:T(1024)}, /*index=5*/f32[768]{0:T(1024)}) all-reduce(f32[768]{0:T(1024)S(1)} %get-tuple-element.19, f32[768]{0:T(1024)S(1)} %get-tuple-element.24, f32[768]{0:T(1024)S(1)} %copy-done.51, ...), channel_id=1, replica_groups=mesh['dp'=8,'mp'=4] {'dp','mp'}, use_global_device_ids=true, to_apply=%region_19.20 | all-reduce | flops 4608 | bytes 36864 | tf_op jit(solution)/shard_map/psum | solution.py:239
  325.8 2.3 add_add_fusion.2
  328.1 184.2 %all-reduce.5.cloned.1.call-done = (f32[768,192]{0,1:T(8,128)}, f32[768,192]{0,1:T(8,128)}, f32[768,192]{0,1:T(8,128)}, f32[192,768]{1,0:T(8,128)}, f32[768,768]{1,0:T(8,128)}, /*index=5*/f32[768,768]{1,0:T(8,128)}) async-done(((f32[768,192]{0,1:T(8,128)}, f32[768,192]{0,1:T(8,128)}, f32[768,192]{0,1:T(8,128)}, f32[192,768]{1,0:T(8,128)}, f32[768,768]{1,0:T(8,128)}, /*index=5*/f32[768,768]{1,0:T(8,128)}), ...) | async-done | bytes 7077904 | tf_op jit(solution)/shard_map/psum | solution.py:224
  512.3 2.1 copy.42
  514.4 1.9 copy.43
  516.3 1.9 copy.44
  519.0 1.4 copy.46
  520.4 1.4 copy.47
  (211 shorter events, 42.5 us)
Async XLA Ops:
  7.2 116.2 %copy-start = (bf16[768,768]{1,0:T(8,128)(2,1)S(1)}, bf16[768,768]{1,0:T(8,128)(2,1)}, u32[]{:S(2)}) copy-start(bf16[768,768]{1,0:T(8,128)(2,1)} %param.35) | copy-start | bytes 3538948
  7.2 29.0 %all-gather.4.cloned.1.call-start = ((), (), s32[]{:S(2)}) async-start(), calls=%async_computation.4 | async-start | bytes 1966080 | tf_op jit(solution)/shard_map/all_gather | solution.py:70
  8.5 5.9 %copy-start.41 = (f32[256]{0:T(256)}, f32[256]{0:T(256)S(1)}, u32[]{:S(2)}) copy-start(f32[256]{0:T(256)S(1)} %broadcast_multiply_fusion.1) | copy-start | bytes 3076
  10.3 4.1 copy-start.46
  10.9 3.4 copy-start.38
  13.7 68.3 %reduce-scatter.5.cloned.1.call-start = ((), (), s32[]{:S(2)}) async-start(), calls=%async_computation.5 | async-start | bytes 1966080 | tf_op jit(solution)/shard_map/reduce_scatter | solution.py:100
  15.0 23.4 %copy-start.35 = (bf16[768,192]{0,1:T(8,128)(2,1)S(1)}, bf16[768,192]{0,1:T(8,128)(2,1)}, u32[]{:S(2)}) copy-start(bf16[768,192]{0,1:T(8,128)(2,1)} %param.26) | copy-start | bytes 884740
  38.5 6.5 %copy-start.16 = (bf16[512,192]{0,1:T(8,128)(2,1)}, bf16[512,192]{0,1:T(8,128)(2,1)S(1)}, u32[]{:S(2)}) copy-start(bf16[512,192]{0,1:T(8,128)(2,1)S(1)} %get-tuple-element.55) | copy-start | bytes 589828
  39.2 5.8 %copy-start.7 = (bf16[1024,192]{0,1:T(8,128)(2,1)}, bf16[1024,192]{0,1:T(8,128)(2,1)S(1)}, u32[]{:S(2)}) copy-start(bf16[1024,192]{0,1:T(8,128)(2,1)S(1)} %convolution_convert_fusion.4) | copy-start | bytes 1179652
  42.8 5.1 copy-start.22
  44.9 6.4 %copy-start.27 = (bf16[3,64,512]{2,1,0:T(8,128)(2,1)}, bf16[3,64,512]{2,1,0:T(8,128)(2,1)S(1)}, u32[]{:S(2)}) copy-start(bf16[3,64,512]{2,1,0:T(8,128)(2,1)S(1)} %fusion.35) | copy-start | bytes 589828
  51.3 4.8 copy-start.11
  51.3 5.7 %copy-start.61 = (bf16[768]{0:T(1024)(128)(2,1)S(1)}, bf16[768]{0:T(1024)(128)(2,1)}, u32[]{:S(2)}) copy-start(bf16[768]{0:T(1024)(128)(2,1)} %param.30) | copy-start | bytes 4612
  51.3 30.6 %copy-start.4 = (bf16[256,768]{1,0:T(8,128)(2,1)S(1)}, bf16[256,768]{1,0:T(8,128)(2,1)}, u32[]{:S(2)}) copy-start(bf16[256,768]{1,0:T(8,128)(2,1)} %param.19) | copy-start | bytes 1179652
  53.8 69.6 %all-gather.6.cloned.1.call-start = ((), (), s32[]{:S(2)}) async-start(), calls=%async_computation.7 | async-start | bytes 1966080 | tf_op jit(solution)/shard_map/all_gather | solution.py:128
  57.0 110.2 %reduce-scatter.9.cloned.1.call-start = ((), (), s32[]{:S(2)}) async-start(), calls=%async_computation.8 | async-start | bytes 1966080 | tf_op jit(solution)/shard_map/reduce_scatter | solution.py:137
  83.2 30.9 %copy-start.45 = (f32[256]{0:T(256)}, f32[256]{0:T(256)S(1)}, u32[]{:S(2)}) copy-start(f32[256]{0:T(256)S(1)} %broadcast_multiply_fusion) | copy-start | bytes 3076
  84.6 34.1 %copy-start.58 = (f32[256]{0:T(256)}, f32[256]{0:T(256)S(1)}, u32[]{:S(2)}) copy-start(f32[256]{0:T(256)S(1)} %multiply_reduce_fusion.2) | copy-start | bytes 3076
  84.6 34.0 %copy-start.52 = (f32[256]{0:T(256)}, f32[256]{0:T(256)S(1)}, u32[]{:S(2)}) copy-start(f32[256]{0:T(256)S(1)} %fusion.54) | copy-start | bytes 3076
  85.9 7.3 %collective-permute-start = (bf16[256,768]{1,0:T(8,128)(2,1)S(1)}, bf16[256,768]{1,0:T(8,128)(2,1)S(1)}, u32[]{:S(2)}, u32[]{:S(2)}) collective-permute-start(bf16[256,768]{1,0:T(8,128)(2,1)S(1)} %add_convert_fusion.3), channel_id=1, source_target_pairs={{0,1},{1,2},{2,3},{3,0},{4,5},{5,6},{6,7},{7,4},{8,9},{9,10},{10,1... | collective-permute-start | bytes 1179656 | tf_op jit(solution)/shard_map/ppermute | solution.py:112
  93.2 13.3 %collective-permute-start.1 = (bf16[256,768]{1,0:T(8,128)(2,1)S(1)}, bf16[256,768]{1,0:T(8,128)(2,1)S(1)}, u32[]{:S(2)}, u32[]{:S(2)}) collective-permute-start(bf16[256,768]{1,0:T(8,128)(2,1)S(1)} %collective-permute-done), channel_id=1, source_target_pairs={{0,1},{1,2},{2,3},{3,0},{4,5},{5,6},{6,7},{7,4},{8,9},{9,10},{10,1... | collective-permute-start | bytes 1179656 | tf_op jit(solution)/shard_map/ppermute | solution.py:112
  106.4 7.6 %collective-permute-start.2 = (bf16[256,768]{1,0:T(8,128)(2,1)S(1)}, bf16[256,768]{1,0:T(8,128)(2,1)S(1)}, u32[]{:S(2)}, u32[]{:S(2)}) collective-permute-start(bf16[256,768]{1,0:T(8,128)(2,1)S(1)} %collective-permute-done.1), channel_id=1, source_target_pairs={{0,1},{1,2},{2,3},{3,0},{4,5},{5,6},{6,7},{7,4},{8,9},{9,10},{10,1... | collective-permute-start | bytes 1179656 | tf_op jit(solution)/shard_map/ppermute | solution.py:112
  123.4 13.0 %copy-start.63 = (bf16[768,768]{1,0:T(8,128)(2,1)S(1)}, bf16[768,768]{1,0:T(8,128)(2,1)}, u32[]{:S(2)}) copy-start(bf16[768,768]{1,0:T(8,128)(2,1)} %param.33) | copy-start | bytes 3538948
  139.0 58.6 %reduce-scatter.7.cloned.1.call-start = ((), (), s32[]{:S(2)}) async-start(), calls=%async_computation.6 | async-start | bytes 1966080 | tf_op jit(solution)/shard_map/reduce_scatter | solution.py:118
  143.5 23.7 %copy-start.6 = (bf16[256,768]{1,0:T(8,128)(2,1)S(1)}, bf16[256,768]{1,0:T(8,128)(2,1)}, u32[]{:S(2)}) copy-start(bf16[256,768]{1,0:T(8,128)(2,1)} %reduce-scatter.5.cloned.1.call-done) | copy-start | bytes 1179652
  146.1 54.1 %copy-start.12 = (bf16[256,768]{1,0:T(8,128)(2,1)S(1)}, bf16[256,768]{1,0:T(8,128)(2,1)}, u32[]{:S(2)}) copy-start(bf16[256,768]{1,0:T(8,128)(2,1)} %param.37) | copy-start | bytes 1179652
  146.1 76.2 %all-gather.8.cloned.1.call-start = ((), (), s32[]{:S(2)}) async-start(), calls=%async_computation.9 | async-start | bytes 1966080 | tf_op jit(solution)/shard_map/all_gather | solution.py:150
  200.2 24.3 %copy-start.23 = (bf16[1024,192]{0,1:T(8,128)(2,1)S(1)}, bf16[1024,192]{0,1:T(8,128)(2,1)}, u32[]{:S(2)}) copy-start(bf16[1024,192]{0,1:T(8,128)(2,1)} %copy-done.22) | copy-start | bytes 1179652
  202.6 78.5 %reduce-scatter.11.cloned.1.call-start = ((), (), s32[]{:S(2)}) async-start(), calls=%async_computation.10 | async-start | bytes 1966080 | tf_op jit(solution)/shard_map/reduce_scatter | solution.py:202
  224.5 4.0 slice-start
  224.5 4.7 slice-start.1
  228.5 3.9 slice-start.2
  229.2 3.2 slice-start.3
  244.8 267.4 %all-reduce.5.cloned.1.call-start = ((), (), s32[]{:S(2)}) async-start(), calls=%async_computation.11 | async-start | bytes 14155776 | tf_op jit(solution)/shard_map/psum | solution.py:224
  245.1 4.9 copy-start.25
  245.1 4.9 copy-start.62
  258.1 23.0 %copy-start.39 = (f32[768]{0:T(1024)S(1)}, f32[768]{0:T(1024)}, u32[]{:S(2)}) copy-start(f32[768]{0:T(1024)} %copy-done.38) | copy-start | bytes 9220
  258.1 23.0 %copy-start.42 = (f32[256]{0:T(256)S(1)}, f32[256]{0:T(256)}, u32[]{:S(2)}) copy-start(f32[256]{0:T(256)} %copy-done.41) | copy-start | bytes 3076
  258.1 24.3 %copy-start.57 = (f32[256]{0:T(256)S(1)}, f32[256]{0:T(256)}, u32[]{:S(2)}) copy-start(f32[256]{0:T(256)} %copy-done.56) | copy-start | bytes 3076
  258.1 24.3 %copy-start.47 = (f32[256]{0:T(256)S(1)}, f32[256]{0:T(256)}, u32[]{:S(2)}) copy-start(f32[256]{0:T(256)} %copy-done.46) | copy-start | bytes 3076
  258.1 25.8 %copy-start.48 = (f32[768]{0:T(1024)S(1)}, f32[768]{0:T(1024)}, u32[]{:S(2)}) copy-start(f32[768]{0:T(1024)} %get-tuple-element.17) | copy-start | bytes 9220
  258.1 25.8 %copy-start.49 = (f32[768]{0:T(1024)S(1)}, f32[768]{0:T(1024)}, u32[]{:S(2)}) copy-start(f32[768]{0:T(1024)} %get-tuple-element.23) | copy-start | bytes 9220
  258.1 25.8 %copy-start.50 = (f32[768]{0:T(1024)S(1)}, f32[768]{0:T(1024)}, u32[]{:S(2)}) copy-start(f32[768]{0:T(1024)} %get-tuple-element.21) | copy-start | bytes 9220
  258.1 25.8 %copy-start.51 = (f32[768]{0:T(1024)S(1)}, f32[768]{0:T(1024)}, u32[]{:S(2)}) copy-start(f32[768]{0:T(1024)} %get-tuple-element.22) | copy-start | bytes 9220
  258.2 67.6 %copy-start.13 = (bf16[256,768]{1,0:T(8,128)(2,1)S(1)}, bf16[256,768]{1,0:T(8,128)(2,1)}, u32[]{:S(2)}) copy-start(bf16[256,768]{1,0:T(8,128)(2,1)} %param.37) | copy-start | bytes 1179652
  258.2 67.6 %copy-start.55 = (f32[256]{0:T(256)S(1)}, f32[256]{0:T(256)}, u32[]{:S(2)}) copy-start(f32[256]{0:T(256)} %copy-done.54) | copy-start | bytes 3076
  512.3 5.9 %copy-start.31 = (f32[192,768]{1,0:T(8,128)S(1)}, f32[192,768]{1,0:T(8,128)}, u32[]{:S(2)}) copy-start(f32[192,768]{1,0:T(8,128)} %get-tuple-element.77) | copy-start | bytes 1769476
  512.3 6.7 %copy-start.15 = (f32[768,768]{1,0:T(8,128)S(1)}, f32[768,768]{1,0:T(8,128)}, u32[]{:S(2)}) copy-start(f32[768,768]{1,0:T(8,128)} %get-tuple-element.81) | copy-start | bytes 7077892
  (32 other events, 57.5 us)
Sparse Core Ops, SparseCore 0:
  13.8 22.3 all-gather.3
  53.9 27.9 reduce-scatter.4
  84.1 22.7 all-gather.5
  139.2 27.9 reduce-scatter.8
  169.6 27.9 reduce-scatter.6
  202.7 19.6 all-gather.7
  245.0 28.0 reduce-scatter.10
  279.3 232.9 all-reduce.4
